TPU v7x, 512 devices: a whole 4x8x8 slice. The times are simulated.
512 devices in a mesh: row: 16 (over x_hi, y), col: 32 (over z, x_lo, core).
Axes of the slice: x: 4 (x_hi: 2, x_lo: 2; x = x_hi * 2 + x_lo), y: 8, z: 8, core: 2. Of those that a mesh axis runs over, the one named last changes fastest.
Arguments:
- base_input: bfloat16 [1024, 16384], P('col', 'row'), may hold values from -6 to 6
- layer_input: bfloat16 [1024, 16384], P('row', 'col'), may hold values from -6 to 6
- out_grad: bfloat16 [1024, 16384], P('col', 'row'), may hold values from -6 to 6
- cross_weight: bfloat16 [16384, 16384], P('row', 'col'), may hold values from -0.046875 to 0.046875
- cross_bias: bfloat16 [16384], P('row'), may hold values from -5 to 5
Outputs:
- weight_grad: float32 [16384, 16384], P('row', 'col')
- bias_grad: float32 [16384], P('row')
- base_grad: bfloat16 [1024, 16384], P('col', 'row')
- branch_grad: bfloat16 [1024, 16384], P('row', 'col')
All inputs are finite; a program needn't handle non-finite values.
Results may differ from a plain program's by a relative error of at most 0.019.
Values may be sent and summed in bfloat16 or wider, within the bound.
A program may use at most 64 MiB of HBM per device.

v0:
```python
import jax
import jax.numpy as jnp
from jax import lax
from jax.sharding import PartitionSpec as P


def on_device(base_input, layer_input, out_grad, cross_weight, cross_bias):
    input_panel = lax.all_gather(layer_input, "row", axis=0, tiled=True)
    grad_panel, base_panel = (
        lax.all_gather(out_grad, "col", axis=0, tiled=True),
        lax.all_gather(base_input, "col", axis=0, tiled=True),
    )
    hidden_panel = (grad_panel.astype(jnp.float32) * base_panel.astype(jnp.float32)).astype(
        jnp.bfloat16
    )
    weight_grad = lax.dot_general(
        hidden_panel, input_panel, (((0,), (0,)), ((), ())), preferred_element_type=jnp.float32
    )
    bias_grad = jnp.sum(hidden_panel, axis=0, dtype=jnp.float32)
    rows = input_panel
    preact = lax.psum_scatter(
        lax.dot_general(
            rows, cross_weight, (((1,), (1,)), ((), ())), preferred_element_type=jnp.float32
        ).astype(jnp.bfloat16),
        "col",
        scatter_dimension=0,
        tiled=True,
    ).astype(jnp.float32)
    preact = preact + cross_bias.astype(jnp.float32)[None, :]
    base_grad = (out_grad.astype(jnp.float32) * preact).astype(jnp.bfloat16)
    rows = hidden_panel
    branch = lax.psum_scatter(
        jnp.dot(rows, cross_weight, preferred_element_type=jnp.float32).astype(jnp.bfloat16),
        "row",
        scatter_dimension=0,
        tiled=True,
    )
    return (weight_grad, bias_grad, base_grad, branch)


def solution(mesh):
    in_specs = (P("col", "row"), P("row", "col"), P("col", "row"), P("row", "col"), P("row"))
    out_specs = (P("row", "col"), P("row"), P("col", "row"), P("row", "col"))
    return jax.shard_map(
        on_device, mesh=mesh, in_specs=in_specs, out_specs=out_specs, check_vma=False
    )
```

profile of v0, /device:TPU:16, one launch (start us, length us, event | category | flops | bytes accessed | tf_op | source)
XLA Modules:
  0.0 573.2 jit_solution(8535226228451038034)
XLA Ops:
  7.2 0.0 copy-start
  7.2 0.0 all-gather.8.cloned.1.call-start
  7.2 0.7 all-gather.8.cloned.1.call-update
  7.9 0.0 all-gather.6.cloned.1.call-start
  8.0 0.7 all-gather.6.cloned.1.call-update
  8.7 0.0 all-gather.4.cloned.1.call-start
  8.7 0.7 all-gather.4.cloned.1.call-update
  9.4 0.0 reduce-scatter.3.cloned.1.call-start
  9.4 89.4 %all-gather.8.cloned.1.call-done = bf16[1024,512]{1,0:T(8,128)(2,1)} async-done(((bf16[64,512]{1,0:T(8,128)(2,1)}), bf16[1024,512]{1,0:T(8,128)(2,1)}) %all-gather.8.cloned.1.call-update) | async-done | bytes 1048592 | tf_op jit(solution)/shard_map/all_gather | solution.py:8
  98.9 0.0 copy-done
  98.9 3.8 convolution_convert_fusion
  102.7 0.0 reduce-scatter.3.cloned.1.call-update
  102.7 0.0 copy-start.4
  102.7 0.0 reduce-scatter.5.cloned.1.call-start
  102.8 63.9 %all-gather.6.cloned.1.call-done = bf16[1024,1024]{1,0:T(8,128)(2,1)} async-done(((bf16[32,1024]{1,0:T(8,128)(2,1)}), bf16[1024,1024]{1,0:T(8,128)(2,1)}) %all-gather.6.cloned.1.call-update) | async-done | bytes 2097168 | tf_op jit(solution)/shard_map/all_gather | solution.py:11
  166.7 69.4 %all-gather.4.cloned.1.call-done = bf16[1024,1024]{1,0:T(8,128)(2,1)} async-done(((bf16[32,1024]{1,0:T(8,128)(2,1)}), bf16[1024,1024]{1,0:T(8,128)(2,1)}) %all-gather.4.cloned.1.call-update) | async-done | bytes 2097168 | tf_op jit(solution)/shard_map/all_gather | solution.py:10
  236.0 0.0 copy-start.1
  236.0 4.6 convolution_convert_fusion.1
  240.7 0.0 reduce-scatter.5.cloned.1.call-update
  240.7 0.0 copy-done.4
  240.7 0.0 copy-done.1
  240.7 0.0 copy-start.2
  240.7 0.0 copy-start.5
  240.8 3.3 convert_reduce_fusion
  244.1 0.0 copy-done.2
  244.1 0.0 copy-done.5
  244.1 0.0 copy-start.3
  244.1 2.6 fusion
  246.7 113.2 %reduce-scatter.3.cloned.1.call-done = bf16[32,1024]{1,0:T(8,128)(2,1)} async-done(((bf16[1024,1024]{1,0:T(8,128)(2,1)}), bf16[32,1024]{1,0:T(8,128)(2,1)}) %reduce-scatter.3.cloned.1.call-update) | async-done | bytes 65552 | tf_op jit(solution)/shard_map/reduce_scatter | solution.py:21
  359.9 0.0 copy-done.3
  359.9 1.5 multiply_convert_fusion.1
  361.4 205.3 %reduce-scatter.5.cloned.1.call-done = bf16[64,512]{1,0:T(8,128)(2,1)} async-done(((bf16[1024,512]{1,0:T(8,128)(2,1)}), bf16[64,512]{1,0:T(8,128)(2,1)}) %reduce-scatter.5.cloned.1.call-update) | async-done | bytes 65552 | tf_op jit(solution)/shard_map/reduce_scatter | solution.py:32
  (1 shorter events, 0.0 us)
Async XLA Ops:
  7.2 91.7 %copy-start = (bf16[1024,512]{1,0:T(8,128)(2,1)S(1)}, bf16[1024,512]{1,0:T(8,128)(2,1)}, u32[]{:S(2)}) copy-start(bf16[1024,512]{1,0:T(8,128)(2,1)} %param.8) | copy-start | bytes 3145732
  7.2 91.7 %all-gather.8.cloned.1.call-start = ((), (), s32[]{:S(2)}) async-start(), calls=%async_computation.4 | async-start | bytes 1114112 | tf_op jit(solution)/shard_map/all_gather | solution.py:8
  7.9 158.7 %all-gather.6.cloned.1.call-start = ((), (), s32[]{:S(2)}) async-start(), calls=%async_computation.3 | async-start | bytes 2162688 | tf_op jit(solution)/shard_map/all_gather | solution.py:11
  8.7 227.4 %all-gather.4.cloned.1.call-start = ((), (), s32[]{:S(2)}) async-start(), calls=%async_computation.2 | async-start | bytes 2162688 | tf_op jit(solution)/shard_map/all_gather | solution.py:10
  9.4 350.5 %reduce-scatter.3.cloned.1.call-start = ((), (), s32[]{:S(2)}) async-start(), calls=%async_computation.5 | async-start | bytes 2162688 | tf_op jit(solution)/shard_map/reduce_scatter | solution.py:21
  102.7 138.0 %copy-start.4 = (bf16[1024]{0:T(1024)(128)(2,1)S(1)}, bf16[1024]{0:T(1024)(128)(2,1)}, u32[]{:S(2)}) copy-start(bf16[1024]{0:T(1024)(128)(2,1)} %param.9) | copy-start | bytes 6148
  102.7 463.9 %reduce-scatter.5.cloned.1.call-start = ((), (), s32[]{:S(2)}) async-start(), calls=%async_computation.6 | async-start | bytes 1114112 | tf_op jit(solution)/shard_map/reduce_scatter | solution.py:32
  236.0 4.7 copy-start.1
  240.7 3.3 copy-start.2
  240.7 3.3 copy-start.5
  244.1 115.8 %copy-start.3 = (bf16[32,1024]{1,0:T(8,128)(2,1)S(1)}, bf16[32,1024]{1,0:T(8,128)(2,1)}, u32[]{:S(2)}) copy-start(bf16[32,1024]{1,0:T(8,128)(2,1)} %param.7) | copy-start | bytes 196612
Sparse Core Ops, SparseCore 0:
  11.2 87.6 all-gather.7
  101.0 65.6 all-gather.5
  168.8 67.1 all-gather.3
  238.7 121.1 reduce-scatter.2
  365.4 201.2 reduce-scatter.4
where the time goes:
time: 573 us
  waiting for transfers between devices  543 us (95%)
  between operations  13.8 us (2%)
  matrix products  11.1 us (2%)
    reduce_scatter x1, waiting for transfers between devices, on_device(): lax.psum_scatter(jnp.dot(rows, cross_weight, preferred_element_type=jnp.f...  205 us
    reduce_scatter x1, waiting for transfers between devices, on_device(): lax.psum_scatter(lax.dot_general(rows, cross_weight, (((1,), (1,)), ((),...  113 us
    all_gather x1, waiting for transfers between devices, on_device(): input_panel = lax.all_gather(layer_input, 'row', axis=0, tiled=True)  89.4 us
    all_gather x1, waiting for transfers between devices, on_device(): lax.all_gather(out_grad, 'col', axis=0, tiled=True)  69.4 us
    all_gather x1, waiting for transfers between devices, on_device(): lax.all_gather(base_input, 'col', axis=0, tiled=True)  63.9 us
  transfers between devices with their start and end apart: 5, of which 5 were waited for; matrix products, arithmetic and copies ran while one was open for 3% of the time, Pallas kernels for 0%

commit v1 on v0

v1 whole, which is shorter than its diff:
```python
import jax
import jax.numpy as jnp
from jax import lax
from jax.experimental import pallas as pl
from jax.experimental.pallas import tpu as pltpu
from jax.sharding import PartitionSpec as P

F32, BF16 = jnp.float32, jnp.bfloat16
NZ = NY = 8
HOPS = 4
PIECES = 4


def cross_backward(
    base_hbm, inp_hbm, grad_hbm, w_hbm, bias_ref,
    wg_hbm, bg_ref, baseg_ref, branch_ref,
    base, grad, w, wt, hid, inp, pre, pre_in, back, wg,
    c_first, c_slot, c_xout, c_xin, r_first, r_slot, r_xout, r_xin,
    in_sem, out_sem,
    cg_s, cg_r, rg_s, rg_r, x_s, x_r, pg_s, pg_r,
    cs_s, cs_r, rs_s, rs_r, ps_s, ps_r, fx_s, fx_r,
):
    row, col = lax.axis_index("row"), lax.axis_index("col")
    xh, y = row // NY, lax.rem(row, NY)
    z, xl, core = col // 4, lax.rem(col // 2, 2), lax.rem(col, 2)

    def col_of(zz, xx, kk):
        return zz * 4 + xx * 2 + kk

    def at_z(d):
        return lax.rem(z + (d + NZ), NZ)

    def at_y(d):
        return lax.rem(y + (d + NY), NY)

    side = (1, -1)
    z_id = [(row, col_of(at_z(d), xl, core)) for d in side]
    y_id = [(xh * NY + at_y(d), col) for d in side]
    xl_id = (row, col_of(z, 1 - xl, core))
    core_id = (row, col_of(z, xl, 1 - core))
    xh_id = ((1 - xh) * NY + y, col)
    xls = (xl, 1 - xl)
    xhs = (xh, 1 - xh)
    sent = []

    def send(src, dst, s_sem, r_sem, to):
        copy = pltpu.make_async_remote_copy(
            src_ref=src, dst_ref=dst, send_sem=s_sem, recv_sem=r_sem,
            device_id=to, device_id_type=pl.DeviceIdType.MESH,
        )
        copy.start()
        sent.append(copy)
        return copy

    loads = [
        pltpu.make_async_copy(grad_hbm, grad, in_sem.at[0]),
        pltpu.make_async_copy(base_hbm, base, in_sem.at[1]),
        pltpu.make_async_copy(inp_hbm, inp.at[row], in_sem.at[2]),
        pltpu.make_async_copy(w_hbm, w, in_sem.at[3]),
    ]
    for load in loads:
        load.start()
    barrier = pltpu.get_barrier_semaphore()
    for to in (*z_id, *y_id, xl_id, core_id, xh_id):
        pl.semaphore_signal(barrier, inc=1, device_id=to, device_id_type=pl.DeviceIdType.MESH)
    loads[0].wait()
    loads[1].wait()
    hid[col] = (grad[...].astype(F32) * base[...].astype(F32)).astype(BF16)
    loads[2].wait()
    pl.semaphore_wait(barrier, 7)

    cg, rg, pg = {}, {}, {}

    def col_block(d, j, s):
        return col_of(at_z(-d * s), xls[j], core)

    def row_block(d, j, s):
        return xhs[j] * NY + at_y(-d * s)

    def half(ref, rows, i, last):
        return ref.at[pl.ds(i * (rows // 2), rows // 2)] if last else ref

    def gather_col(i, j, s):
        blk = half(hid.at[col_block(side[i], j, s - 1)], 32, i, s == HOPS)
        cg[i, j, s] = send(blk, blk, cg_s.at[i, j, s - 1], cg_r.at[i, j, s - 1], z_id[i])

    def gather_row(i, j, s):
        blk = half(inp.at[row_block(side[i], j, s - 1)], 64, i, s == HOPS)
        rg[i, j, s] = send(blk, blk, rg_s.at[i, j, s - 1], rg_r.at[i, j, s - 1], y_id[i])

    def share(zz, j, n):
        blk = hid.at[col_of(zz, xls[j], core)]
        pg[n, j] = send(blk, blk, pg_s.at[n, j], pg_r.at[n, j], core_id)

    x_col = send(hid.at[col], hid.at[col], x_s.at[0], x_r.at[0], xl_id)
    x_row = send(inp.at[row], inp.at[row], x_s.at[1], x_r.at[1], xh_id)
    for i in range(2):
        gather_col(i, 0, 1)
        gather_row(i, 0, 1)
    share(z, 0, 0)
    loads[3].wait()
    wt[...] = w[...].T
    x_col.wait_recv()
    for i in range(2):
        gather_col(i, 1, 1)
    share(z, 1, 0)
    x_row.wait_recv()
    for i in range(2):
        gather_row(i, 1, 1)

    ps = {}

    def pre_rows(ys):
        blocks = [xx * NY + yy for yy in ys for xx in (0, 1)]
        lhs = jnp.concatenate([inp[b] for b in blocks], axis=0)
        part = jnp.dot(lhs, wt[...], preferred_element_type=F32).astype(BF16)
        for n, b in enumerate(blocks):
            pre[b] = part[n * 64 : (n + 1) * 64]

    def merge_out(ys, base_n):
        n = base_n
        for yy in ys:
            for xx in (0, 1):
                b = xx * NY + yy
                ps[n] = send(
                    pre.at[b, pl.ds((1 - core) * 32, 32)], pre_in.at[b], ps_s.at[n], ps_r.at[n], core_id
                )
                n += 1

    def back_rows(zs):
        lhs = jnp.concatenate([hid[pl.ds(zz * 4, 4)].reshape(128, 1024) for zz in zs], axis=0)
        part = jnp.dot(lhs, w[...], preferred_element_type=F32).astype(BF16)
        for n, zz in enumerate(zs):
            back[pl.ds(zz * 2, 2)] = part[n * 128 : (n + 1) * 128].reshape(2, 64, 512)

    pre_rows([y])
    merge_out([y], 0)
    for s in range(1, HOPS + 1):
        for j in range(2):
            for i in range(2):
                cg[i, j, s].wait_recv()
                if s < HOPS:
                    gather_col(i, j, s + 1)
                    share(at_z(-side[i] * s), j, 2 * s - 1 + i)
            if s == HOPS:
                share(at_z(HOPS), j, 7)
            for i in range(2):
                rg[i, j, s].wait_recv()
                if s < HOPS:
                    gather_row(i, j, s + 1)
        if s < HOPS:
            pre_rows([at_y(-s), at_y(s)])
            merge_out([at_y(-s), at_y(s)], 2 + 4 * (s - 1))
            if s == 1:
                for j in range(2):
                    pg[0, j].wait_recv()
                back_rows([z])
            else:
                for j in range(2):
                    pg[2 * s - 3, j].wait_recv()
                    pg[2 * s - 2, j].wait_recv()
                back_rows([at_z(-(s - 1)), at_z(s - 1)])
    pre_rows([at_y(HOPS)])
    merge_out([at_y(HOPS)], 14)
    for j in range(2):
        pg[5, j].wait_recv()
        pg[6, j].wait_recv()
        pg[7, j].wait_recv()
    back_rows([at_z(-3), at_z(3), at_z(HOPS)])
    for n in range(16):
        ps[n].wait_recv()

    cs, rs = {}, {}
    mine = pl.ds(pl.multiple_of(core * 32, 32), 32)

    def pre_sum(zz, j, rows=None):
        b = zz * 2 + xls[j]
        if rows is None:
            return pre[b, mine].astype(F32) + pre_in[b].astype(F32)
        start, size = rows
        return pre[b, pl.ds(pl.multiple_of(core * 32 + start, 16), size)].astype(F32) + pre_in[
            b, pl.ds(start, size)
        ].astype(F32)

    def scatter_col(i, j, s):
        zz = at_z(side[i] * (HOPS + 1 - s))
        if s == 1:
            src, dst = c_first.at[i, j], c_slot.at[i, j, 0, pl.ds(i * 16, 16)]
            c_first[i, j] = pre_sum(zz, j, (i * 16, 16)).astype(BF16)
        else:
            slot = c_slot.at[i, j, s - 2]
            src, dst = slot, c_slot.at[i, j, s - 1]
            if s == 2:
                o = 1 - i
                own = pre_sum(zz, j, (i * 16, 16)) + slot[pl.ds(i * 16, 16)].astype(F32)
                slot[pl.ds(i * 16, 16)] = own.astype(BF16)
                slot[pl.ds(o * 16, 16)] = pre_sum(zz, j, (o * 16, 16)).astype(BF16)
            else:
                slot[...] = (pre_sum(zz, j) + slot[...].astype(F32)).astype(BF16)
        cs[i, j, s] = send(src, dst, cs_s.at[i, j, s - 1], cs_r.at[i, j, s - 1], z_id[i])

    def scatter_row(i, j, s):
        b = xhs[j] * NY + at_y(side[i] * (HOPS + 1 - s))
        if s == 1:
            src, dst = r_first.at[i, j], r_slot.at[i, j, 0, pl.ds(i * 32, 32)]
            r_first[i, j] = back[b, pl.ds(i * 32, 32)]
        else:
            slot = r_slot.at[i, j, s - 2]
            src, dst = slot, r_slot.at[i, j, s - 1]
            if s == 2:
                mid, oth = pl.ds(i * 32, 32), pl.ds((1 - i) * 32, 32)
                slot[mid] = (back[b, mid].astype(F32) + slot[mid].astype(F32)).astype(BF16)
                slot[oth] = back[b, oth]
            else:
                slot[...] = (back[b].astype(F32) + slot[...].astype(F32)).astype(BF16)
        rs[i, j, s] = send(src, dst, rs_s.at[i, j, s - 1], rs_r.at[i, j, s - 1], y_id[i])

    for j in (1, 0):
        for i in range(2):
            scatter_col(i, j, 1)
        for i in range(2):
            scatter_row(i, j, 1)

    outs = []
    width = 1024 // PIECES

    def weight_piece(n):
        cols = slice(n * width, (n + 1) * width)
        lhs = hid[:, :, cols].reshape(1024, width)
        wg[cols] = lax.dot_general(
            lhs, inp[...].reshape(1024, 512), (((0,), (0,)), ((), ())), preferred_element_type=F32
        )
        copy = pltpu.make_async_copy(wg.at[cols], wg_hbm.at[cols], out_sem.at[n])
        copy.start()
        outs.append(copy)

    weight_piece(0)
    for s in range(1, HOPS):
        for j in (1, 0):
            for i in range(2):
                cs[i, j, s].wait_recv()
                scatter_col(i, j, s + 1)
            for i in range(2):
                rs[i, j, s].wait_recv()
                scatter_row(i, j, s + 1)
        weight_piece(s)
    bg_ref[...] = jnp.sum(
        jnp.sum(hid[...].reshape(128, 8, 1024).astype(F32), axis=0), axis=0, keepdims=True
    )

    def col_total(j):
        total = pre_sum(z, j)
        for i in range(2):
            cs[i, j, HOPS].wait_recv()
            total = total + c_slot[i, j, HOPS - 1].astype(F32)
        return total

    def row_total(j):
        total = back[xhs[j] * NY + y].astype(F32)
        for i in range(2):
            rs[i, j, HOPS].wait_recv()
            total = total + r_slot[i, j, HOPS - 1].astype(F32)
        return total

    c_xout[...] = col_total(1).astype(BF16)
    fx_col = send(c_xout, c_xin, fx_s.at[0], fx_r.at[0], xl_id)
    r_xout[...] = row_total(1).astype(BF16)
    fx_row = send(r_xout, r_xin, fx_s.at[1], fx_r.at[1], xh_id)
    preact = col_total(0)
    branch = row_total(0)
    fx_col.wait_recv()
    preact = preact + c_xin[...].astype(F32) + bias_ref[...].astype(F32)
    baseg_ref[...] = (grad[...].astype(F32) * preact).astype(BF16)
    fx_row.wait_recv()
    branch_ref[...] = (branch + r_xin[...].astype(F32)).astype(BF16)
    for copy in outs:
        copy.wait()
    for copy in sent:
        copy.wait_send()


def on_device(base_input, layer_input, out_grad, cross_weight, cross_bias):
    dma = pltpu.SemaphoreType.DMA
    hbm, vmem = pl.BlockSpec(memory_space=pl.ANY), pl.BlockSpec(memory_space=pltpu.VMEM)
    weight_grad, bias_grad, base_grad, branch_grad = pl.pallas_call(
        cross_backward,
        out_shape=(
            jax.ShapeDtypeStruct((1024, 512), F32),
            jax.ShapeDtypeStruct((1, 1024), F32),
            jax.ShapeDtypeStruct((32, 1024), BF16),
            jax.ShapeDtypeStruct((64, 512), BF16),
        ),
        in_specs=[hbm, hbm, hbm, hbm, vmem],
        out_specs=(hbm, vmem, vmem, vmem),
        scratch_shapes=[
            pltpu.VMEM((32, 1024), BF16),
            pltpu.VMEM((32, 1024), BF16),
            pltpu.VMEM((1024, 512), BF16),
            pltpu.VMEM((512, 1024), BF16),
            pltpu.VMEM((32, 32, 1024), BF16),
            pltpu.VMEM((16, 64, 512), BF16),
            pltpu.VMEM((16, 64, 1024), BF16),
            pltpu.VMEM((16, 32, 1024), BF16),
            pltpu.VMEM((16, 64, 512), BF16),
            pltpu.VMEM((1024, 512), F32),
            pltpu.VMEM((2, 2, 16, 1024), BF16),
            pltpu.VMEM((2, 2, 4, 32, 1024), BF16),
            pltpu.VMEM((32, 1024), BF16),
            pltpu.VMEM((32, 1024), BF16),
            pltpu.VMEM((2, 2, 32, 512), BF16),
            pltpu.VMEM((2, 2, 4, 64, 512), BF16),
            pltpu.VMEM((64, 512), BF16),
            pltpu.VMEM((64, 512), BF16),
            dma((4,)), dma((PIECES,)),
            dma((2, 2, 4)), dma((2, 2, 4)), dma((2, 2, 4)), dma((2, 2, 4)), dma((2,)), dma((2,)), dma((8, 2)), dma((8, 2)),
            dma((2, 2, 4)), dma((2, 2, 4)), dma((2, 2, 4)), dma((2, 2, 4)), dma((16,)), dma((16,)), dma((2,)), dma((2,)),
        ],
        compiler_params=pltpu.CompilerParams(
            collective_id=0, has_side_effects=True, vmem_limit_bytes=40 << 20
        ),
    )(base_input, layer_input, out_grad, cross_weight, cross_bias.reshape(1, 1024))
    return weight_grad, bias_grad.reshape(1024), base_grad, branch_grad


def solution(mesh):
    in_specs = (P("col", "row"), P("row", "col"), P("col", "row"), P("row", "col"), P("row"))
    out_specs = (P("row", "col"), P("row"), P("col", "row"), P("row", "col"))
    return jax.shard_map(
        on_device, mesh=mesh, in_specs=in_specs, out_specs=out_specs, check_vma=False
    )
```

time: 573 us -> 64.5 us (0.11)
  waiting for transfers between devices: 543 us -> 0 us
  Pallas kernels: 0 us -> 56 us
  between operations: 13.8 us -> 0.64 us
  matrix products: 11.1 us -> 0 us
  local copies, waits for them, and re-layouts: 0.03 us -> 7.6 us
    reduce_scatter x2 -> x0, waiting for transfers between devices: 318 us -> none  [the longest x1 205 us: on_device(): lax.psum_scatter(jnp.dot(rows, cross_weight, preferred_element_type=jnp.f...]
    all_gather x3 -> x0, waiting for transfers between devices: 223 us -> none  [the longest x1 89.4 us: on_device(): input_panel = lax.all_gather(layer_input, 'row', axis=0, tiled=True)]
    pallas_call x0 -> x1, Pallas kernels: none -> 56 us  [on_device(): pl.pallas_call(cross_backward, out_shape=(jax.ShapeDtypeStruct((1024, 512...]
    dot_general x3 -> x0, matrix products: 11.1 us -> none  [the longest x1 4.65 us: on_device(): jnp.dot(rows, cross_weight, preferred_element_type=jnp.float32)]
    unnamed x12, local copies, waits for them, and re-layouts: 0.03 us -> 6.91 us
  transfers between devices with their start and end apart: 5 -> 0, of which waited for: 5 -> 0; matrix products, arithmetic and copies ran while one was open for 3% -> 0% of each run, Pallas kernels for 0% -> 0%
where the time goes in v1:
time: 64.5 us; the launch traced here: 64.2 us
  Pallas kernels  56 us (87%)
  local copies, waits for them, and re-layouts  7.6 us (12%)
    pallas_call x1, Pallas kernels, on_device(): pl.pallas_call(cross_backward, out_shape=(jax.ShapeDtypeStruct((1024, 512...  56 us
    unnamed x12, local copies, waits for them, and re-layouts  6.91 us

profile of v1, /device:TPU:16, one launch (start us, length us, event | category | flops | bytes accessed | tf_op | source)
XLA Modules:
  0.0 64.2 jit_solution(11491560269468314541)
XLA Ops:
  0.6 0.7 %reshape.14.bias_ref = bf16[1,1024]{1,0:T(2,128)(2,1)S(1)} reshape(bf16[1024]{0:T(1024)(128)(2,1)} %param.9) | data formatting | bytes 4096 | tf_op jit(solution)/shard_map/reshape | solution.py:321
  1.3 0.0 copy-start
  1.3 1.2 %copy-done = bf16[1024,512]{1,0:T(8,128)(2,1)S(1)} copy-done((bf16[1024,512]{1,0:T(8,128)(2,1)S(1)}, bf16[1024,512]{1,0:T(8,128)(2,1)}, u32[]{:S(2)}) %copy-start) | copy-done | bytes 1048600
  2.5 0.0 copy-start.1
  2.5 0.8 %copy-done.1 = bf16[32,1024]{1,0:T(8,128)(2,1)S(1)} copy-done((bf16[32,1024]{1,0:T(8,128)(2,1)S(1)}, bf16[32,1024]{1,0:T(8,128)(2,1)}, u32[]{:S(2)}) %copy-start.1) | copy-done | bytes 65560
  3.4 0.0 copy-start.2
  3.4 0.8 %copy-done.2 = bf16[64,512]{1,0:T(8,128)(2,1)S(1)} copy-done((bf16[64,512]{1,0:T(8,128)(2,1)S(1)}, bf16[64,512]{1,0:T(8,128)(2,1)}, u32[]{:S(2)}) %copy-start.2) | copy-done | bytes 65560
  4.2 0.0 copy-start.3
  4.2 0.8 %copy-done.3 = bf16[32,1024]{1,0:T(8,128)(2,1)S(1)} copy-done((bf16[32,1024]{1,0:T(8,128)(2,1)S(1)}, bf16[32,1024]{1,0:T(8,128)(2,1)}, u32[]{:S(2)}) %copy-start.3) | copy-done | bytes 65560
  5.1 56.0 %shard_map.84 = (f32[1024,512]{1,0:T(8,128)S(1)}, f32[1,1024]{1,0:T(1,128)S(1)}, bf16[32,1024]{1,0:T(8,128)(2,1)S(1)}, bf16[64,512]{1,0:T(8,128)(2,1)S(1)}) custom-call(bf16[32,1024]{1,0:T(8,128)(2,1)S(1)} %copy-done.1, bf16[64,512]{1,0:T(8,128)(2,1)S(1)} %copy-done.2, bf16[32,1024]{1,0:T(8,128)(2,1)S(1)} %copy-done.3, bf16[1024,512]{1,0:T(8,128)(2,1)S(1)} %copy-done, ...), custom_call_target="tpu_custom_call" | custom-call | tf_op jit(solution)/shard_map/pallas_call | solution.py:285
  61.0 1.3 %copy.13 = f32[1024,512]{1,0:T(8,128)} copy(f32[1024,512]{1,0:T(8,128)S(1)} %get-tuple-element.16) | data formatting | bytes 4194304
  62.4 0.6 copy.14
  63.0 0.6 copy.15
  63.6 0.6 copy.16
Async XLA Ops:
  1.3 1.2 %copy-start = (bf16[1024,512]{1,0:T(8,128)(2,1)S(1)}, bf16[1024,512]{1,0:T(8,128)(2,1)}, u32[]{:S(2)}) copy-start(bf16[1024,512]{1,0:T(8,128)(2,1)} %w_hbm.1) | copy-start | bytes 3145732
  2.5 0.8 %copy-start.1 = (bf16[32,1024]{1,0:T(8,128)(2,1)S(1)}, bf16[32,1024]{1,0:T(8,128)(2,1)}, u32[]{:S(2)}) copy-start(bf16[32,1024]{1,0:T(8,128)(2,1)} %base_hbm.1) | copy-start | bytes 196612
  3.4 0.8 %copy-start.2 = (bf16[64,512]{1,0:T(8,128)(2,1)S(1)}, bf16[64,512]{1,0:T(8,128)(2,1)}, u32[]{:S(2)}) copy-start(bf16[64,512]{1,0:T(8,128)(2,1)} %inp_hbm.1) | copy-start | bytes 196612
  4.2 0.8 %copy-start.3 = (bf16[32,1024]{1,0:T(8,128)(2,1)S(1)}, bf16[32,1024]{1,0:T(8,128)(2,1)}, u32[]{:S(2)}) copy-start(bf16[32,1024]{1,0:T(8,128)(2,1)} %grad_hbm.1) | copy-start | bytes 196612

commit v2 on v0

v2 whole, which is shorter than its diff:
```python
import jax
import jax.numpy as jnp
from jax import lax
from jax.experimental import pallas as pl
from jax.experimental.pallas import tpu as pltpu
from jax.sharding import PartitionSpec as P

F32, BF16 = jnp.float32, jnp.bfloat16
NZ = NY = 8
HOPS = 4
PIECES = 8


def cross_backward(
    base_hbm, inp_hbm, grad_hbm, w_hbm, bias_hbm,
    wg_ref, bg_ref, baseg_ref, branch_ref,
    base, grad, w, wt, hid, inp, pre, pre_in, back, bias,
    c_slot, c_xout, c_xin, r_slot, r_xout, r_xin,
    in_sem,
    cg_s, cg_r, rg_s, rg_r, x_s, x_r, pg_s, pg_r,
    cs_s, cs_r, rs_s, rs_r, ps_s, ps_r, fx_s, fx_r,
):
    row, col = lax.axis_index("row"), lax.axis_index("col")
    xh, y = row // NY, lax.rem(row, NY)
    z, xl, core = col // 4, lax.rem(col // 2, 2), lax.rem(col, 2)

    def col_of(zz, xx, kk):
        return zz * 4 + xx * 2 + kk

    def at_z(d):
        return lax.rem(z + (d + NZ), NZ)

    def at_y(d):
        return lax.rem(y + (d + NY), NY)

    side = (1, -1)
    z_id = [(row, col_of(at_z(d), xl, core)) for d in side]
    y_id = [(xh * NY + at_y(d), col) for d in side]
    xl_id = (row, col_of(z, 1 - xl, core))
    core_id = (row, col_of(z, xl, 1 - core))
    xh_id = ((1 - xh) * NY + y, col)
    xls = (xl, 1 - xl)
    xhs = (xh, 1 - xh)
    sent = []

    def send(src, dst, s_sem, r_sem, to):
        copy = pltpu.make_async_remote_copy(
            src_ref=src, dst_ref=dst, send_sem=s_sem, recv_sem=r_sem,
            device_id=to, device_id_type=pl.DeviceIdType.MESH,
        )
        copy.start()
        sent.append(copy)
        return copy

    loads = [
        pltpu.make_async_copy(grad_hbm, grad, in_sem.at[0]),
        pltpu.make_async_copy(base_hbm, base, in_sem.at[1]),
        pltpu.make_async_copy(inp_hbm, inp.at[row], in_sem.at[2]),
        pltpu.make_async_copy(w_hbm, w, in_sem.at[3]),
        pltpu.make_async_copy(bias_hbm, bias, in_sem.at[4]),
    ]
    for load in loads:
        load.start()
    barrier = pltpu.get_barrier_semaphore()
    for to in (*z_id, *y_id, xl_id, core_id, xh_id):
        pl.semaphore_signal(barrier, inc=1, device_id=to, device_id_type=pl.DeviceIdType.MESH)
    loads[0].wait()
    loads[1].wait()
    hid[col] = (grad[...].astype(F32) * base[...].astype(F32)).astype(BF16)
    loads[2].wait()
    pl.semaphore_wait(barrier, 7)

    cg, rg, pg, ps = {}, {}, {}, {}
    order = [(j, q) for j in range(2) for q in range(2)]

    def col_part(ref, q):
        return ref.at[pl.ds(q * 16, 16)]

    def row_part(ref, q):
        return ref.at[pl.ds(q * 32, 32)]

    def dirs(q, last):
        return (q,) if last else (0, 1)

    def gather_col(i, j, q, s):
        blk = col_part(hid.at[col_of(at_z(-side[i] * (s - 1)), xls[j], core)], q)
        cg[i, j, q, s] = send(blk, blk, cg_s.at[i, j, q, s - 1], cg_r.at[i, j, q, s - 1], z_id[i])

    def gather_row(i, j, q, s):
        blk = row_part(inp.at[xhs[j] * NY + at_y(-side[i] * (s - 1))], q)
        rg[i, j, q, s] = send(blk, blk, rg_s.at[i, j, q, s - 1], rg_r.at[i, j, q, s - 1], y_id[i])

    def share(zz, j, n):
        blk = hid.at[col_of(zz, xls[j], core)]
        pg[n, j] = send(blk, blk, pg_s.at[n, j], pg_r.at[n, j], core_id)

    def arrive(j, q, s):
        for i in dirs(q, s == HOPS):
            cg[i, j, q, s].wait_recv()
            if s < HOPS and i in dirs(q, s + 1 == HOPS):
                gather_col(i, j, q, s + 1)
        if q == 1:
            if s == HOPS:
                share(at_z(HOPS), j, 7)
            else:
                for i in range(2):
                    share(at_z(-side[i] * s), j, 2 * s - 1 + i)
        for i in dirs(q, s == HOPS):
            rg[i, j, q, s].wait_recv()
            if s < HOPS and i in dirs(q, s + 1 == HOPS):
                gather_row(i, j, q, s + 1)

    def pre_rows(ys, base_n):
        blocks = [xx * NY + yy for yy in ys for xx in (0, 1)]
        lhs = jnp.concatenate([inp[b] for b in blocks], axis=0)
        part = jnp.dot(lhs, wt[...], preferred_element_type=F32).astype(BF16)
        for n, b in enumerate(blocks):
            pre[b] = part[n * 64 : (n + 1) * 64]
        for n, b in enumerate(blocks, base_n):
            ps[n] = send(
                pre.at[b, pl.ds((1 - core) * 32, 32)], pre_in.at[b], ps_s.at[n], ps_r.at[n], core_id
            )

    def back_rows(zs, shares):
        for n in shares:
            for j in range(2):
                pg[n, j].wait_recv()
        lhs = jnp.concatenate([hid[pl.ds(zz * 4, 4)].reshape(128, 1024) for zz in zs], axis=0)
        part = jnp.dot(lhs, w[...], preferred_element_type=F32).astype(BF16)
        for n, zz in enumerate(zs):
            back[pl.ds(zz * 2, 2)] = part[n * 128 : (n + 1) * 128].reshape(2, 64, 512)

    for q in range(2):
        for i in range(2):
            gather_col(i, 0, q, 1)
            gather_row(i, 0, q, 1)
    x_col, x_row = {}, {}
    for q in range(2):
        blk = col_part(hid.at[col], q)
        x_col[q] = send(blk, blk, x_s.at[0, q], x_r.at[0, q], xl_id)
        blk = row_part(inp.at[row], q)
        x_row[q] = send(blk, blk, x_s.at[1, q], x_r.at[1, q], xh_id)
    share(z, 0, 0)
    loads[3].wait()
    loads[4].wait()
    wt[...] = w[...].T
    for c in range(HOPS + 1):
        if c < HOPS:
            for q in range(2):
                arrive(0, q, c + 1)
        if c == 1:
            pre_rows([y], 0)
        elif c > 1:
            pre_rows([at_y(1 - c), at_y(c - 1)], 4 * c - 6)
        for q in range(2):
            if c == 0:
                x_col[q].wait_recv()
                for i in range(2):
                    gather_col(i, 1, q, 1)
                if q == 1:
                    share(z, 1, 0)
                x_row[q].wait_recv()
                for i in range(2):
                    gather_row(i, 1, q, 1)
            else:
                arrive(1, q, c)
        if c == 1:
            back_rows([z], [0])
        elif c > 1 and c < HOPS:
            back_rows([at_z(1 - c), at_z(c - 1)], [2 * c - 3, 2 * c - 2])
    pre_rows([at_y(HOPS)], 14)
    back_rows([at_z(-3), at_z(3), at_z(HOPS)], [5, 6, 7])

    cs, rs = {}, {}

    def pre_sum(zz, j, q):
        b = zz * 2 + xls[j]
        own = pre[b, pl.ds(pl.multiple_of(core * 32 + q * 16, 16), 16)]
        return own.astype(F32) + pre_in[b, pl.ds(q * 16, 16)].astype(F32)

    def scatter_col(i, j, q, s):
        slot = c_slot.at[i, j, q, s - 1]
        total = pre_sum(at_z(side[i] * (HOPS + 1 - s)), j, q)
        if s > 2 or (s == 2 and q == i):
            cs[i, j, q, s - 1].wait_recv()
            total = total + slot[...].astype(F32)
        slot[...] = total.astype(BF16)
        cs[i, j, q, s] = send(
            slot, c_slot.at[i, j, q, s], cs_s.at[i, j, q, s - 1], cs_r.at[i, j, q, s - 1], z_id[i]
        )

    def scatter_row(i, j, q, s):
        slot = r_slot.at[i, j, q, s - 1]
        own = back[xhs[j] * NY + at_y(side[i] * (HOPS + 1 - s)), pl.ds(q * 32, 32)]
        if s > 2 or (s == 2 and q == i):
            rs[i, j, q, s - 1].wait_recv()
            own = (own.astype(F32) + slot[...].astype(F32)).astype(BF16)
        slot[...] = own
        rs[i, j, q, s] = send(
            slot, r_slot.at[i, j, q, s], rs_s.at[i, j, q, s - 1], rs_r.at[i, j, q, s - 1], y_id[i]
        )

    width = 1024 // PIECES

    def weight_piece(n):
        cols = slice(n * width, (n + 1) * width)
        lhs = hid[:, :, cols].reshape(1024, width)
        wg_ref[cols] = lax.dot_general(
            lhs, inp[...].reshape(1024, 512), (((0,), (0,)), ((), ())), preferred_element_type=F32
        )

    for j in (1, 0):
        for i in range(2):
            scatter_row(i, j, i, 1)
    for n in range(16):
        ps[n].wait_recv()
    for j in (1, 0):
        for i in range(2):
            scatter_col(i, j, i, 1)
    for j in (1, 0):
        for i in range(2):
            scatter_col(i, j, 1 - i, 2)
            scatter_row(i, j, 1 - i, 2)
    weight_piece(0)
    weight_piece(1)
    for s in range(2, HOPS + 1):
        for j in (1, 0):
            for q in range(2):
                for i in range(2):
                    if s > 2 or q == i:
                        scatter_col(i, j, q, s)
                for i in range(2):
                    if s > 2 or q == i:
                        scatter_row(i, j, q, s)
            weight_piece(2 * s - 2 + (1 - j))

    def col_total(j, q):
        total = pre_sum(z, j, q)
        for i in range(2):
            cs[i, j, q, HOPS].wait_recv()
            total = total + c_slot[i, j, q, HOPS].astype(F32)
        return total

    def row_total(j, q):
        total = back[xhs[j] * NY + y, pl.ds(q * 32, 32)].astype(F32)
        for i in range(2):
            rs[i, j, q, HOPS].wait_recv()
            total = total + r_slot[i, j, q, HOPS].astype(F32)
        return total

    fx_col, fx_row = {}, {}
    for q in range(2):
        col_part(c_xout, q)[...] = col_total(1, q).astype(BF16)
        fx_col[q] = send(col_part(c_xout, q), col_part(c_xin, q), fx_s.at[0, q], fx_r.at[0, q], xl_id)
        row_part(r_xout, q)[...] = row_total(1, q).astype(BF16)
        fx_row[q] = send(row_part(r_xout, q), row_part(r_xin, q), fx_s.at[1, q], fx_r.at[1, q], xh_id)
    bg_ref[...] = jnp.sum(jnp.sum(hid[...].reshape(128, 8, 1024).astype(F32), axis=0), axis=0)
    preact = [col_total(0, q) for q in range(2)]
    branch = [row_total(0, q) for q in range(2)]
    for q in range(2):
        part = pl.ds(q * 16, 16)
        fx_col[q].wait_recv()
        total = preact[q] + c_xin[part].astype(F32) + bias[...].astype(F32)[None]
        baseg_ref[part] = (grad[part].astype(F32) * total).astype(BF16)
    for q in range(2):
        part = pl.ds(q * 32, 32)
        fx_row[q].wait_recv()
        branch_ref[part] = (branch[q] + r_xin[part].astype(F32)).astype(BF16)
    for copy in sent:
        copy.wait_send()


def write_out(*refs):
    sems = refs[8]
    copies = [pltpu.make_async_copy(refs[n], refs[4 + n], sems.at[n]) for n in range(4)]
    for copy in copies:
        copy.start()
    for copy in copies:
        copy.wait()


OUT_SHAPES = (
    jax.ShapeDtypeStruct((1024, 512), F32),
    jax.ShapeDtypeStruct((1024,), F32),
    jax.ShapeDtypeStruct((32, 1024), BF16),
    jax.ShapeDtypeStruct((64, 512), BF16),
)


def on_device(*args):
    dma = pltpu.SemaphoreType.DMA
    hbm, vmem = pl.BlockSpec(memory_space=pltpu.HBM), pl.BlockSpec(memory_space=pltpu.VMEM)
    any_space = pl.BlockSpec(memory_space=pl.ANY)
    results = pl.pallas_call(
        cross_backward,
        out_shape=OUT_SHAPES,
        in_specs=[hbm] * 5,
        out_specs=(vmem,) * 4,
        scratch_shapes=[
            pltpu.VMEM((32, 1024), BF16),
            pltpu.VMEM((32, 1024), BF16),
            pltpu.VMEM((1024, 512), BF16),
            pltpu.VMEM((512, 1024), BF16),
            pltpu.VMEM((32, 32, 1024), BF16),
            pltpu.VMEM((16, 64, 512), BF16),
            pltpu.VMEM((16, 64, 1024), BF16),
            pltpu.VMEM((16, 32, 1024), BF16),
            pltpu.VMEM((16, 64, 512), BF16),
            pltpu.VMEM((1024,), BF16),
            pltpu.VMEM((2, 2, 2, 5, 16, 1024), BF16),
            pltpu.VMEM((32, 1024), BF16),
            pltpu.VMEM((32, 1024), BF16),
            pltpu.VMEM((2, 2, 2, 5, 32, 512), BF16),
            pltpu.VMEM((64, 512), BF16),
            pltpu.VMEM((64, 512), BF16),
            dma((5,)),
            dma((2, 2, 2, 4)), dma((2, 2, 2, 4)), dma((2, 2, 2, 4)), dma((2, 2, 2, 4)), dma((2, 2)), dma((2, 2)), dma((8, 2)), dma((8, 2)),
            dma((2, 2, 2, 4)), dma((2, 2, 2, 4)), dma((2, 2, 2, 4)), dma((2, 2, 2, 4)), dma((16,)), dma((16,)), dma((2, 2)), dma((2, 2)),
        ],
        compiler_params=pltpu.CompilerParams(
            collective_id=0, has_side_effects=True, vmem_limit_bytes=40 << 20
        ),
    )(*(pltpu.with_memory_space_constraint(a, pltpu.HBM) for a in args))
    return pl.pallas_call(
        write_out,
        out_shape=OUT_SHAPES,
        in_specs=[any_space] * 4,
        out_specs=(any_space,) * 4,
        scratch_shapes=[dma((4,))],
    )(*(pltpu.with_memory_space_constraint(a, pltpu.VMEM) for a in results))


def solution(mesh):
    in_specs = (P("col", "row"), P("row", "col"), P("col", "row"), P("row", "col"), P("row"))
    out_specs = (P("row", "col"), P("row"), P("col", "row"), P("row", "col"))
    return jax.shard_map(
        on_device, mesh=mesh, in_specs=in_specs, out_specs=out_specs, check_vma=False
    )
```

time: 573 us -> 56.8 us (0.10)
  waiting for transfers between devices: 543 us -> 0 us
  Pallas kernels: 0 us -> 56.1 us
  between operations: 13.8 us -> 0.64 us
  matrix products: 11.1 us -> 0 us
    reduce_scatter x2 -> x0, waiting for transfers between devices: 318 us -> none  [the longest x1 205 us: on_device(): lax.psum_scatter(jnp.dot(rows, cross_weight, preferred_element_type=jnp.f...]
    all_gather x3 -> x0, waiting for transfers between devices: 223 us -> none  [the longest x1 89.4 us: on_device(): input_panel = lax.all_gather(layer_input, 'row', axis=0, tiled=True)]
    pallas_call x0 -> x2, Pallas kernels: none -> 56.1 us  [the longest x1 54.7 us: on_device(): pl.pallas_call(cross_backward, out_shape=OUT_SHAPES, in_specs=[hbm] * 5,...]
    dot_general x3 -> x0, matrix products: 11.1 us -> none  [the longest x1 4.65 us: on_device(): jnp.dot(rows, cross_weight, preferred_element_type=jnp.float32)]
  transfers between devices with their start and end apart: 5 -> 0, of which waited for: 5 -> 0; matrix products, arithmetic and copies ran while one was open for 3% -> 0% of each run, Pallas kernels for 0% -> 0%
where the time goes in v2:
time: 56.8 us; the launch traced here: 56.7 us
  Pallas kernels  56.1 us (99%)
  between operations  0.64 us (1%)
    pallas_call x1, Pallas kernels, on_device(): pl.pallas_call(cross_backward, out_shape=OUT_SHAPES, in_specs=[hbm] * 5,...  54.7 us
    pallas_call x1, Pallas kernels, on_device(): pl.pallas_call(write_out, out_shape=OUT_SHAPES, in_specs=[any_space] * 4,...  1.38 us

profile of v2, /device:TPU:16, one launch (start us, length us, event | category | flops | bytes accessed | tf_op | source)
XLA Modules:
  0.0 56.7 jit_solution(13630365572993740974)
XLA Ops:
  0.6 54.7 %shard_map.84 = (f32[1024,512]{1,0:T(8,128)S(1)}, f32[1024]{0:T(1024)S(1)}, bf16[32,1024]{1,0:T(8,128)(2,1)S(1)}, bf16[64,512]{1,0:T(8,128)(2,1)S(1)}) custom-call(bf16[32,1024]{1,0:T(8,128)(2,1)} %base_hbm.1, bf16[64,512]{1,0:T(8,128)(2,1)} %inp_hbm.1, bf16[32,1024]{1,0:T(8,128)(2,1)} %grad_hbm.1, bf16[1024,512]{1,0:T(8,128)(2,1)} %w_hbm.1, ...), custom_call_target="tpu_custom_call" | custom-call | tf_op jit(solution)/shard_map/pallas_call | solution.py:294
  55.3 1.4 %shard_map.85 = (f32[1024,512]{1,0:T(8,128)}, f32[1024]{0:T(1024)}, bf16[32,1024]{1,0:T(8,128)(2,1)}, bf16[64,512]{1,0:T(8,128)(2,1)}) custom-call(f32[1024,512]{1,0:T(8,128)S(1)} %get-tuple-element.8.refs_0_, f32[1024]{0:T(1024)S(1)} %get-tuple-element.9.refs_1_, bf16[32,1024]{1,0:T(8,128)(2,1)S(1)} %get-tuple-element.10.refs_2_, ...), custom_call_target="tpu_custom_call" | custom-call | tf_op jit(solution)/shard_map/pallas_call | solution.py:324
